TPU v7x, 32 devices: a whole 2x2x4 slice. The times are simulated.
32 devices in a mesh: ctx: 8 (over z, x), tp: 4 (over y, core).
Axes of the slice: x: 2, y: 2, z: 4, core: 2. Of those that a mesh axis runs over, the one named last changes fastest.
Arguments:
- inputs: bfloat16 [4096, 768], P(('ctx', 'tp')), may hold values from -6 to 6
- positions: int32 [4096], P('ctx'), may hold values from 0 to 3071, as said below
- attn_scale: float32 [768], replicated, may hold values from 0.1 to 1.9
- attn_shift: float32 [768], replicated, may hold values from -4 to 4
- mlp_scale: float32 [768], replicated, may hold values from 0.1 to 1.9
- mlp_shift: float32 [768], replicated, may hold values from -4 to 4
- qkv_weight: bfloat16 [768, 3, 768], P(None, None, 'tp'), may hold values from -0.21875 to 0.21875
- qv_bias: float32 [2, 768], P(None, 'tp'), may hold values from -4 to 4
- dense_weight: bfloat16 [768, 768], P('tp'), may hold values from -1.75 to 1.75
- dense_bias: float32 [768], replicated, may hold values from -5 to 5
- up_weight: bfloat16 [768, 3072], P(None, 'tp'), may hold values from -0.21875 to 0.21875
- up_bias: float32 [3072], P('tp'), may hold values from -4 to 4
- down_weight: bfloat16 [3072, 768], P('tp'), may hold values from -0.109375 to 0.109375
- down_bias: float32 [768], replicated, may hold values from -5 to 5
- cotangent: bfloat16 [4096, 768], P(('ctx', 'tp')), may hold values from -6 to 6
Outputs:
- output: bfloat16 [4096, 768], P(('ctx', 'tp'))
- grad_input: float32 [4096, 768], P(('ctx', 'tp'))
- grad_attn_scale: float32 [768], replicated
- grad_attn_shift: float32 [768], replicated
- grad_mlp_scale: float32 [768], replicated
- grad_mlp_shift: float32 [768], replicated
- grad_qkv: float32 [768, 3, 768], P(None, None, 'tp')
- grad_qv_bias: float32 [2, 768], P(None, 'tp')
- grad_dense: float32 [768, 768], P('tp')
- grad_dense_bias: float32 [768], replicated
- grad_up: float32 [768, 3072], P(None, 'tp')
- grad_up_bias: float32 [3072], P('tp')
- grad_down: float32 [3072, 768], P('tp')
- grad_down_bias: float32 [768], replicated
Inputs may be any that keep to these rules, and one draw needn't show every extreme that they name: The sequence holds three documents; positions count from 0 at each document's first token and rise by one along it; the second document has 3072 tokens and starts at a token between 1 and 1023.
All inputs are finite; a program needn't handle non-finite values.
Results may differ from a plain program's by a relative error of at most 0.025.
Values may be sent and summed in bfloat16 or wider, within the bound.
A program may use at most 128 MiB of HBM per device.

v0:
```python
import math
import jax
import jax.numpy as jnp
from jax import lax
from jax.sharding import PartitionSpec as P

D = 768
HD = 64
ROT = 16
norm_eps = 1e-05


def layer_norm(values, scale, shift):
    mean_value = jnp.mean(values, axis=-1, keepdims=True)
    centred = values - mean_value
    variance = jnp.mean(centred * centred, axis=-1, keepdims=True)
    inv_std = lax.rsqrt(variance + norm_eps)
    normal_part = centred * inv_std
    return (normal_part * scale + shift, normal_part, inv_std)


def norm_backward(grad_normed, normal_part, inv_std, scale):
    grad_hat = grad_normed * scale
    mean_grad = jnp.mean(grad_hat, axis=-1, keepdims=True)
    mean_mixed = jnp.mean(grad_hat * normal_part, axis=-1, keepdims=True)
    return inv_std * (grad_hat - mean_grad - normal_part * mean_mixed)


def rotary_tables(positions):
    freqs = 10000.0 ** (-jnp.arange(0, ROT, 2).astype(jnp.float32) / ROT)
    angles = positions.astype(jnp.float32)[:, None] * freqs[None, :]
    angles = jnp.concatenate([angles, angles], axis=1)
    return (jnp.cos(angles), jnp.sin(angles))


def rotate(tensor, cosines, sines):
    part = tensor[..., :ROT]
    half = ROT // 2
    turned = jnp.concatenate([-part[..., half:], part[..., :half]], axis=-1)
    spun = part * cosines[:, None, :] + turned * sines[:, None, :]
    return jnp.concatenate([spun, tensor[..., ROT:]], axis=-1)


def gelu_grad(pre_act):
    cumulative = 0.5 * (1.0 + jax.scipy.special.erf(pre_act * 0.7071067811865476))
    density = jnp.exp(-0.5 * pre_act * pre_act) * 0.3989422804014327
    return cumulative + pre_act * density


def block_length(length):
    return math.gcd(length, 1024)


def local(
    inputs,
    positions,
    attn_scale,
    attn_shift,
    mlp_scale,
    mlp_shift,
    qkv_weight,
    qv_bias,
    dense_weight,
    dense_bias,
    up_weight,
    up_bias,
    down_weight,
    down_bias,
    cotangent,
):
    local_width = qkv_weight.shape[2]
    head_count = local_width // HD
    score_scale = HD ** (-0.5)
    resid = inputs.astype(jnp.float32)
    normed_one, hat_one, std_one = layer_norm(resid, attn_scale, attn_shift)
    normed_two, hat_two, std_two = layer_norm(resid, mlp_scale, mlp_shift)
    attn_in, mlp_in = (
        lax.all_gather(normed_one.astype(jnp.bfloat16), "tp", axis=0, tiled=True),
        lax.all_gather(normed_two.astype(jnp.bfloat16), "tp", axis=0, tiled=True),
    )
    block_rows = attn_in.shape[0]
    proj = jnp.dot(
        attn_in, qkv_weight.reshape(D, 3 * local_width), preferred_element_type=jnp.float32
    )
    proj = proj.reshape(block_rows, 3, head_count, HD)
    cosines, sines = rotary_tables(positions)
    queries = rotate(proj[:, 0] + qv_bias[0].reshape(head_count, HD), cosines, sines).astype(
        jnp.bfloat16
    )
    keys_rot = rotate(proj[:, 1], cosines, sines).astype(jnp.bfloat16)
    values = (proj[:, 2] + qv_bias[1].reshape(head_count, HD)).astype(jnp.bfloat16)
    own_start = lax.axis_index("ctx") * block_rows
    query_pos = own_start + jnp.arange(block_rows, dtype=jnp.int32)
    first_key = query_pos - positions
    last_query = query_pos[block_rows - 1]
    earliest_key = jnp.min(first_key)

    def visible_mask(start_row, length):
        key_pos = start_row + jnp.arange(length, dtype=jnp.int32)
        return (key_pos[None, :] <= query_pos[:, None]) & (key_pos[None, :] >= first_key[:, None])

    def reachable(start_row, length):
        return (start_row <= last_query) & (start_row + length - 1 >= earliest_key)

    def attend_block(running, key_block, value_block, start_row):
        row_max, row_sum, accumulated = running
        visible = visible_mask(start_row, key_block.shape[0])
        scores = (
            jnp.einsum("qhd,khd->hqk", queries, key_block, preferred_element_type=jnp.float32)
            * score_scale
        )
        scores = jnp.where(visible[None], scores, -1e30)
        new_max = jnp.maximum(row_max, jnp.max(scores, axis=-1))
        weights = jnp.where(visible[None], jnp.exp(scores - new_max[..., None]), 0.0)
        factor = jnp.exp(row_max - new_max)
        row_sum = row_sum * factor + jnp.sum(weights, axis=-1)
        accumulated = accumulated * factor[..., None] + jnp.einsum(
            "hqk,khd->hqd",
            weights.astype(jnp.bfloat16),
            value_block,
            preferred_element_type=jnp.float32,
        )
        return (new_max, row_sum, accumulated)

    initial = (
        jnp.full((head_count, block_rows), -1e30, jnp.float32),
        jnp.zeros((head_count, block_rows), jnp.float32),
        jnp.zeros((head_count, block_rows, HD), jnp.float32),
    )
    running = initial
    key_rows = lax.all_gather(keys_rot, "ctx", axis=0, tiled=True)
    value_rows = lax.all_gather(values, "ctx", axis=0, tiled=True)
    length = key_rows.shape[0]
    attend_step_rows = block_length(length)
    steps_count = length // attend_step_rows
    key_blocks = key_rows.reshape(steps_count, attend_step_rows, head_count, HD)
    value_blocks = value_rows.reshape(steps_count, attend_step_rows, head_count, HD)

    def one_step(current, inputs_step):
        key_block, value_block, number = inputs_step
        block_start = number * attend_step_rows

        def attend_now(state):
            return attend_block(state, key_block, value_block, block_start)

        def keep_state(state):
            return state

        return (
            lax.cond(reachable(block_start, attend_step_rows), attend_now, keep_state, current),
            None,
        )

    running, unused = lax.scan(
        one_step, running, (key_blocks, value_blocks, jnp.arange(steps_count, dtype=jnp.int32))
    )
    row_max, row_sum, accumulated = running
    attended = jnp.transpose(accumulated / row_sum[..., None], (1, 0, 2)).astype(jnp.bfloat16)
    log_total = row_max + jnp.log(row_sum)
    attended_flat = attended.reshape(block_rows, local_width)
    attn_part = jnp.dot(attended_flat, dense_weight, preferred_element_type=jnp.float32)
    pre_act = jnp.dot(mlp_in, up_weight, preferred_element_type=jnp.float32) + up_bias
    activation = jax.nn.gelu(pre_act, approximate=False).astype(jnp.bfloat16)
    mlp_part = jnp.dot(activation, down_weight, preferred_element_type=jnp.float32)
    branch_sum = lax.psum_scatter(attn_part + mlp_part, "tp", scatter_dimension=0, tiled=True)
    output = (resid + branch_sum + dense_bias + down_bias).astype(jnp.bfloat16)
    grad_out = cotangent.astype(jnp.float32)
    bias_grad = jnp.sum(grad_out, axis=0)
    grad_full = lax.all_gather(cotangent, "tp", axis=0, tiled=True)
    grad_down = jnp.dot(activation.T, grad_full, preferred_element_type=jnp.float32)
    grad_act = jnp.dot(grad_full, down_weight.T, preferred_element_type=jnp.float32)
    grad_pre = grad_act * gelu_grad(pre_act)
    grad_up_bias = jnp.sum(grad_pre, axis=0)
    grad_pre_low = grad_pre.astype(jnp.bfloat16)
    grad_up = jnp.dot(mlp_in.T, grad_pre_low, preferred_element_type=jnp.float32)
    grad_mlp_in = jnp.dot(grad_pre_low, up_weight.T, preferred_element_type=jnp.float32)
    grad_dense = jnp.dot(attended_flat.T, grad_full, preferred_element_type=jnp.float32)
    grad_attended = jnp.dot(grad_full, dense_weight.T, preferred_element_type=jnp.float32)
    grad_attended = grad_attended.astype(jnp.bfloat16).reshape(block_rows, head_count, HD)
    delta_rows = jnp.transpose(
        jnp.sum(grad_attended.astype(jnp.float32) * attended.astype(jnp.float32), axis=-1)
    )

    def score_grads(query_rows, grad_rows, log_rows, delta_part, key_block, value_block, visible):
        scores = (
            jnp.einsum("qhd,khd->hqk", query_rows, key_block, preferred_element_type=jnp.float32)
            * score_scale
        )
        weights = jnp.where(visible[None], jnp.exp(scores - log_rows[..., None]), 0.0)
        grad_weights = jnp.einsum(
            "qhd,khd->hqk", grad_rows, value_block, preferred_element_type=jnp.float32
        )
        grad_scores = (weights * (grad_weights - delta_part[..., None])).astype(jnp.bfloat16)
        return (weights.astype(jnp.bfloat16), grad_scores)

    key_back, value_back = (
        lax.all_gather(keys_rot, "ctx", axis=0, tiled=True),
        lax.all_gather(values, "ctx", axis=0, tiled=True),
    )
    total_rows = key_back.shape[0]
    step_rows = block_length(total_rows)
    steps_count = total_rows // step_rows
    back_inputs = (
        key_back.reshape(steps_count, step_rows, head_count, HD),
        value_back.reshape(steps_count, step_rows, head_count, HD),
        jnp.arange(steps_count, dtype=jnp.int32),
    )
    zero_query = jnp.zeros((block_rows, head_count, HD), jnp.float32)

    def back_step(query_grad, inputs_step):
        key_block, value_block, number = inputs_step
        block_start = number * step_rows

        def with_terms(grad_now):
            visible = visible_mask(block_start, step_rows)
            weights_low, grad_scores = score_grads(
                queries, grad_attended, log_total, delta_rows, key_block, value_block, visible
            )
            grad_now = (
                grad_now
                + jnp.einsum(
                    "hqk,khd->qhd", grad_scores, key_block, preferred_element_type=jnp.float32
                )
                * score_scale
            )
            key_part = (
                jnp.einsum("hqk,qhd->khd", grad_scores, queries, preferred_element_type=jnp.float32)
                * score_scale
            )
            value_part = jnp.einsum(
                "hqk,qhd->khd", weights_low, grad_attended, preferred_element_type=jnp.float32
            )
            joined = jnp.concatenate(
                [
                    key_part.reshape(step_rows, local_width),
                    value_part.reshape(step_rows, local_width),
                ],
                axis=1,
            )
            return (grad_now, joined)

        def without_terms(grad_now):
            return (grad_now, jnp.zeros((step_rows, 2 * local_width), jnp.float32))

        return lax.cond(reachable(block_start, step_rows), with_terms, without_terms, query_grad)

    query_grad, key_terms = lax.scan(back_step, zero_query, back_inputs)
    key_terms = key_terms.reshape(total_rows, 2 * local_width)
    own_terms = lax.psum_scatter(key_terms, "ctx", scatter_dimension=0, tiled=True)
    key_grad = own_terms[:, :local_width].reshape(block_rows, head_count, HD)
    value_grad = own_terms[:, local_width:].reshape(block_rows, head_count, HD)
    grad_query_pre = rotate(query_grad, cosines, -sines)
    grad_key_pre = rotate(key_grad, cosines, -sines)
    qv_bias_grad = jnp.stack(
        [
            jnp.sum(grad_query_pre, axis=0).reshape(local_width),
            jnp.sum(value_grad, axis=0).reshape(local_width),
        ]
    )
    grad_proj = jnp.stack([grad_query_pre, grad_key_pre, value_grad], axis=1)
    grad_proj = grad_proj.reshape(block_rows, 3 * local_width).astype(jnp.bfloat16)
    grad_qkv = jnp.dot(attn_in.T, grad_proj, preferred_element_type=jnp.float32).reshape(
        D, 3, local_width
    )
    grad_attn_in = jnp.dot(
        grad_proj, qkv_weight.reshape(D, 3 * local_width).T, preferred_element_type=jnp.float32
    )
    own_attn, own_mlp = (
        lax.psum_scatter(grad_attn_in, "tp", scatter_dimension=0, tiled=True),
        lax.psum_scatter(grad_mlp_in, "tp", scatter_dimension=0, tiled=True),
    )
    grad_input = grad_out + norm_backward(own_attn, hat_one, std_one, attn_scale)
    grad_input = grad_input + norm_backward(own_mlp, hat_two, std_two, mlp_scale)
    norm_sums = lax.psum(
        (
            jnp.sum(own_attn * hat_one, axis=0),
            jnp.sum(own_attn, axis=0),
            jnp.sum(own_mlp * hat_two, axis=0),
            jnp.sum(own_mlp, axis=0),
            bias_grad,
        ),
        ("ctx", "tp"),
    )
    weight_sums = lax.psum(
        (grad_qkv, qv_bias_grad, grad_dense, grad_up, grad_up_bias, grad_down), "ctx"
    )
    return (
        output,
        grad_input,
        norm_sums[0],
        norm_sums[1],
        norm_sums[2],
        norm_sums[3],
        weight_sums[0],
        weight_sums[1],
        weight_sums[2],
        norm_sums[4],
        weight_sums[3],
        weight_sums[4],
        weight_sums[5],
        norm_sums[4],
    )


def solution(mesh):
    in_specs = (
        P(("ctx", "tp"), None),
        P("ctx"),
        P(),
        P(),
        P(),
        P(),
        P(None, None, "tp"),
        P(None, "tp"),
        P("tp", None),
        P(),
        P(None, "tp"),
        P("tp"),
        P("tp", None),
        P(),
        P(("ctx", "tp"), None),
    )
    out_specs = (
        P(("ctx", "tp"), None),
        P(("ctx", "tp"), None),
        P(),
        P(),
        P(),
        P(),
        P(None, None, "tp"),
        P(None, "tp"),
        P("tp", None),
        P(),
        P(None, "tp"),
        P("tp"),
        P("tp", None),
        P(),
    )
    return jax.shard_map(local, mesh=mesh, in_specs=in_specs, out_specs=out_specs, check_vma=False)
```

profile of v0, /device:TPU:0, one launch (start us, length us, event | category | flops | bytes accessed | tf_op | source)
XLA Modules:
  0.0 690.6 jit_solution(9488253124478135631)
XLA Ops:
  7.3 1.2 convert_reduce_fusion
  8.5 1.1 fusion.84
  9.6 1.9 fusion.74
  11.5 10.1 %all_gather.17 = bf16[512,768]{1,0:T(8,128)(2,1)S(1)} all-gather(bf16[128,768]{1,0:T(8,128)(2,1)S(1)} %get-tuple-element.958), channel_id=1, replica_groups=mesh['ctx'=8,'tp'=4] {'tp'}, dimensions={0}, use_global_device_ids=true | all-gather | bytes 983040 | tf_op jit(solution)/shard_map/all_gather | solution.py:78
  23.5 1.2 fusion.107
  27.7 8.7 %all_gather.21 = bf16[512,768]{1,0:T(8,128)(2,1)S(1)} all-gather(bf16[128,768]{1,0:T(8,128)(2,1)S(1)} %copy-done.29), channel_id=1, replica_groups=mesh['ctx'=8,'tp'=4] {'tp'}, dimensions={0}, use_global_device_ids=true | all-gather | bytes 983040 | tf_op jit(solution)/shard_map/all_gather | solution.py:169
  37.7 33.9 %all-gather.3.cloned.1.call-done = bf16[4096,3,64]{0,2,1:T(8,128)(2,1)} async-done(((bf16[512,3,64]{0,2,1:T(8,128)(2,1)}), bf16[4096,3,64]{0,2,1:T(8,128)(2,1)}) %all-gather.3.cloned.1.call-update) | async-done | bytes 1572880 | tf_op jit(solution)/shard_map/all_gather | solution.py:131
  71.6 1.6 copy.75
  73.2 43.7 %all-gather.5.cloned.1.call-done = bf16[4096,3,64]{0,2,1:T(8,128)(2,1)} async-done(((bf16[512,3,64]{0,2,1:T(8,128)(2,1)}), bf16[4096,3,64]{0,2,1:T(8,128)(2,1)}) %all-gather.5.cloned.1.call-update) | async-done | bytes 1572880 | tf_op jit(solution)/shard_map/all_gather | solution.py:132
  116.9 2.7 copy.74
  120.1 23.0 %while.39 = (s32[]{:T(128)}, f32[3,512]{1,0:T(4,128)S(1)}, f32[3,512]{1,0:T(4,128)S(1)}, f32[3,512,64]{1,2,0:T(8,128)S(1)}, s32[4]{0:T(128)}, /*index=5*/s32[]{:...) while((s32[]{:T(128)}, f32[3,512]{1,0:T(4,128)S(1)}, ...), condition=%wide.region_8.9_spmd.clone, body=%wide.region_3.8_spmd.clone.sunk | while | flops 424874496 | bytes 22858608 | solution.py:154
  120.1 1.2 dynamic_slice.82
  123.9 7.8 %conditional.6 = ((f32[3,512]{1,0:T(4,128)S(1)}, f32[3,512]{1,0:T(4,128)S(1)}, f32[3,512,64]{1,2,0:T(8,128)S(1)})) conditional(s32[]{:T(128)} %convert_element_type.207, (f32[3,512]{1,0:T(4,128)S(1)}, f32[3,512]{1,0:T(4,128)S(1)}, f32[3,512,64]{1,2,0:T(8,128)S(1)}) %tuple.156, (s32[]{:T(128)}, s32[]{:T(128)}, s32[512]{0:T(512)}, ...), branch_computations={%region_4.4_spmd, %region_5.7_spmd} | conditional | flops 424874496 | bytes 22856236 | solution.py:150
  124.6 1.2 compare_and_fusion
  125.8 1.4 fusion.4
  127.2 1.6 fusion.6
  128.8 3.0 fusion.10
  131.8 1.2 dynamic_slice.82
  135.6 1.2 dynamic_slice.82
  139.3 1.2 dynamic_slice.82
  143.7 1.4 multiply_reduce_fusion
  145.1 37.2 %while.40 = (s32[]{:T(128)}, f32[512,3,64]{0,2,1:T(8,128)S(1)}, f32[4,1024,384]{2,1,0:T(8,128)}, s32[4]{0:T(128)S(1)}, s32[]{:T(128)}, /*index=5*/s32[]{:T(128)}...) while((s32[]{:T(128)}, f32[512,3,64]{0,2,1:T(8,128)S(1)}, ...), condition=%wide.region_14.15_spmd.clone, body=%wide.region_11.14_spmd.clone.sunk | while | flops 1024722432 | bytes 56325616 | solution.py:247
  147.8 8.3 %conditional.7 = (f32[512,3,64]{0,2,1:T(8,128)S(1)}, f32[1,1024,384]{1,2,0:T(8,128)S(1)}) conditional(s32[]{:T(128)} %convert_element_type.208, f32[512,3,64]{0,2,1:T(8,128)S(1)} %get-tuple-element.1217, (s32[]{:T(128)}, s32[]{:T(128)}, s32[512]{0:T(512)}, bf16[4,1024,3,64]{1,3,2,0:T(8,128)(2,1)S(1)}, s32[]{:T(128)}, ...), branch_computations={%region_12.12_spmd, %region_13.13_spmd} | conditional | flops 1024722432 | bytes 37448308 | solution.py:245
  147.8 1.0 fusion.32
  149.4 3.3 fusion.23
  153.4 1.5 fusion.25
  154.9 1.1 convolution_multiply_fusion
  156.1 1.6 copy.77
  157.7 2.8 constant_dynamic-update-slice_fusion.2
  163.4 1.6 copy.77
  165.0 2.8 constant_dynamic-update-slice_fusion.2
  170.6 1.6 copy.77
  172.3 2.8 constant_dynamic-update-slice_fusion.2
  177.9 1.6 copy.77
  179.5 2.8 constant_dynamic-update-slice_fusion.2
  183.3 8.7 %all_gather.20 = bf16[512,768]{1,0:T(8,128)(2,1)S(1)} all-gather(bf16[128,768]{1,0:T(8,128)(2,1)S(1)} %copy-done.31), channel_id=1, replica_groups=mesh['ctx'=8,'tp'=4] {'tp'}, dimensions={0}, use_global_device_ids=true | all-gather | bytes 983040 | tf_op jit(solution)/shard_map/all_gather | solution.py:79
  192.0 4.2 fusion.44
  196.3 1.1 fusion.109
  198.3 2.0 fusion.93
  201.8 144.9 %reduce-scatter.7.cloned.1.call-done = f32[512,384]{1,0:T(8,128)} async-done(((f32[4096,384]{1,0:T(8,128)}), f32[512,384]{1,0:T(8,128)}) %reduce-scatter.7.cloned.1.call-update) | async-done | bytes 786448 | tf_op jit(solution)/shard_map/reduce_scatter | solution.py:249
  346.7 2.0 slice.122
  348.6 1.8 copy.47
  350.4 1.0 slice_reduce_fusion.2
  351.4 1.3 copy.46
  352.7 0.9 fusion.97
  354.5 2.0 fusion.111
  357.9 2.0 convolution_add_fusion
  360.0 1.1 copy-done.8
  361.0 3.3 fusion.91
  364.4 2.2 fusion.113
  366.6 1.2 fusion.112
  368.1 1.8 fusion.59
  370.0 0.9 copy-done.15
  371.1 20.6 %all-reduce.1 = (f32[2,192]{1,0:T(2,128)}, f32[768]{0:T(1024)}) all-reduce(f32[2,192]{1,0:T(2,128)S(1)} %pad_maximum_fusion.4, f32[768]{0:T(1024)S(1)} %get-tuple-element.970), channel_id=1, replica_groups=mesh['ctx'=8,'tp'=4] {'ctx'}, use_global_device_ids=true, to_apply=%region_33.34 | all-reduce | flops 1152 | bytes 9216 | tf_op jit(solution)/shard_map/psum | solution.py:284
  391.7 15.1 %reduce-scatter.9.cloned.1.call-done = f32[128,768]{1,0:T(8,128)} async-done(((f32[512,768]{1,0:T(8,128)}), f32[128,768]{1,0:T(8,128)}) %reduce-scatter.9.cloned.1.call-update) | async-done | bytes 393232 | tf_op jit(solution)/shard_map/reduce_scatter | solution.py:269
  406.8 1.5 fusion.82
  408.3 28.8 %reduce-scatter.5.cloned.1.call-done = f32[128,768]{1,0:T(8,128)} async-done(((f32[512,768]{1,0:T(8,128)}), f32[128,768]{1,0:T(8,128)}) %reduce-scatter.5.cloned.1.call-update) | async-done | bytes 393232 | tf_op jit(solution)/shard_map/reduce_scatter | solution.py:165
  437.2 2.3 convert_reduce_fusion.1
  439.5 43.0 %all-reduce = (f32[768]{0:T(1024)}, f32[768]{0:T(1024)}, f32[768]{0:T(1024)}, f32[768]{0:T(1024)}, f32[768]{0:T(1024)S(1)}) all-reduce(f32[768]{0:T(1024)S(1)} %get-tuple-element.862, f32[768]{0:T(1024)S(1)} %get-tuple-element.867, f32[768]{0:T(1024)S(1)} %get-tuple-element.871, ...), channel_id=1, replica_groups=mesh['ctx'=8,'tp'=4] {'ctx','tp'}, use_global_device_ids=true, to_apply=%region_23.24 | all-reduce | flops 3840 | bytes 30720 | tf_op jit(solution)/shard_map/psum | solution.py:274
  482.5 193.0 %all-reduce.5.cloned.1.call-done = (f32[768,3,192]{0,2,1:T(8,128)}, f32[192,768]{1,0:T(8,128)}, f32[768,768]{1,0:T(8,128)}, f32[768,768]{1,0:T(8,128)}) async-done(((f32[768,3,192]{0,2,1:T(8,128)}, f32[192,768]{1,0:T(8,128)}, f32[768,768]{1,0:T(8,128)}, f32[768,768]{1,0:T(8,128)}), (f32[768,3,192]{0,2,1:T(8,128)}, f32[192,768]{1,0:T(8,128)}, f32[768,768]{1,0:T(8,128)}, ...) | async-done | bytes 7077904 | tf_op jit(solution)/shard_map/psum | solution.py:284
  676.0 2.9 copy.118
  679.8 1.4 copy.120
  681.2 1.1 copy-done.16
  682.3 1.4 copy.121
  (205 shorter events, 23.2 us)
Async XLA Ops:
  7.2 184.8 %copy-start = (bf16[768,768]{1,0:T(8,128)(2,1)S(1)}, bf16[768,768]{1,0:T(8,128)(2,1)}, u32[]{:S(2)}) copy-start(bf16[768,768]{1,0:T(8,128)(2,1)} %param.33) | copy-start | bytes 3538948
  7.2 14.4 %copy-start.12 = (bf16[768,3,192]{0,2,1:T(8,128)(2,1)S(1)}, bf16[768,3,192]{0,2,1:T(8,128)(2,1)}, u32[]{:S(2)}) copy-start(bf16[768,3,192]{0,2,1:T(8,128)(2,1)} %param.29) | copy-start | bytes 2654212
  7.2 64.4 %all-gather.3.cloned.1.call-start = ((), (), s32[]{:S(2)}) async-start(), calls=%async_computation.4 | async-start | bytes 1769472 | tf_op jit(solution)/shard_map/all_gather | solution.py:131
  8.5 13.1 %copy-start.41 = (f32[128]{0:T(128)}, f32[128]{0:T(128)S(1)}, u32[]{:S(2)}) copy-start(f32[128]{0:T(128)S(1)} %broadcast_multiply_fusion.5) | copy-start | bytes 1540
  9.6 12.0 %copy-start.44 = (f32[128]{0:T(128)}, f32[128]{0:T(128)S(1)}, u32[]{:S(2)}) copy-start(f32[128]{0:T(128)S(1)} %add_rsqrt_fusion) | copy-start | bytes 1540
  21.6 0.9 copy-start.5
  21.6 0.9 copy-start.50
  22.2 1.2 copy-start.49
  23.5 4.2 copy-start.29
  24.8 12.5 %copy-start.23 = (bf16[192,768]{1,0:T(8,128)(2,1)S(1)}, bf16[192,768]{1,0:T(8,128)(2,1)}, u32[]{:S(2)}) copy-start(bf16[192,768]{1,0:T(8,128)(2,1)} %param.31) | copy-start | bytes 884740
  25.5 12.2 %copy-start.34 = (f32[512,16]{0,1:T(8,128)}, f32[512,16]{0,1:T(8,128)S(1)}, u32[]{:S(2)}) copy-start(f32[512,16]{0,1:T(8,128)S(1)} %get-tuple-element.966) | copy-start | bytes 98308
  26.2 90.6 %all-gather.5.cloned.1.call-start = ((), (), s32[]{:S(2)}) async-start(), calls=%async_computation.5 | async-start | bytes 1769472 | tf_op jit(solution)/shard_map/all_gather | solution.py:132
  27.0 319.7 %reduce-scatter.7.cloned.1.call-start = ((), (), s32[]{:S(2)}) async-start(), calls=%async_computation.7 | async-start | bytes 7077888 | tf_op jit(solution)/shard_map/reduce_scatter | solution.py:249
  36.4 0.9 copy-start.3
  145.1 2.7 copy-start.1
  147.8 1.1 copy-start.37
  147.8 1.6 copy-start.40
  147.8 1.6 copy-start.43
  157.7 2.8 copy-start.2
  160.5 2.6 copy-start.1
  165.0 2.8 copy-start.2
  167.8 2.6 copy-start.1
  172.2 2.8 copy-start.2
  175.0 2.6 copy-start.1
  179.5 2.8 copy-start.2
  182.3 0.9 copy-start.31
  182.3 9.7 %copy-start.51 = (f32[768]{0:T(1024)S(1)}, f32[768]{0:T(1024)}, u32[]{:S(2)}) copy-start(f32[768]{0:T(1024)} %param.34) | copy-start | bytes 9220
  182.4 209.3 %reduce-scatter.11.cloned.1.call-start = ((), (), s32[]{:S(2)}) async-start(), calls=%async_computation.9 | async-start | bytes 1966080 | tf_op jit(solution)/shard_map/reduce_scatter | solution.py:270
  192.0 4.3 copy-start.7
  192.0 4.3 copy-start.4
  192.0 4.3 copy-start.21
  197.4 0.9 copy-start.32
  200.3 0.8 copy-start.35
  200.3 0.8 copy-start.36
  200.3 206.5 %reduce-scatter.9.cloned.1.call-start = ((), (), s32[]{:S(2)}) async-start(), calls=%async_computation.8 | async-start | bytes 1966080 | tf_op jit(solution)/shard_map/reduce_scatter | solution.py:269
  200.4 0.7 copy-start.14
  346.7 3.7 copy-start.18
  351.3 2.2 copy-start.27
  351.4 2.2 copy-start.28
  352.6 1.9 copy-start.13
  353.7 0.8 copy-start.9
  354.5 2.1 copy-start.19
  354.5 2.1 copy-start.24
  356.5 80.7 %reduce-scatter.5.cloned.1.call-start = ((), (), s32[]{:S(2)}) async-start(), calls=%async_computation.6 | async-start | bytes 1966080 | tf_op jit(solution)/shard_map/reduce_scatter | solution.py:165
  356.6 1.3 copy-start.22
  359.9 1.1 copy-start.8
  359.9 315.5 %all-reduce.5.cloned.1.call-start = ((), (), s32[]{:S(2)}) async-start(), calls=%async_computation.10 | async-start | bytes 14155776 | tf_op jit(solution)/shard_map/psum | solution.py:284
  364.4 2.2 copy-start.20
  366.6 1.2 copy-start.6
  366.6 1.5 copy-start.10
  369.9 1.0 copy-start.15
  369.9 1.0 copy-start.26
  369.9 36.9 %copy-start.11 = (bf16[128,768]{1,0:T(8,128)(2,1)S(1)}, bf16[128,768]{1,0:T(8,128)(2,1)}, u32[]{:S(2)}) copy-start(bf16[128,768]{1,0:T(8,128)(2,1)} %param.23) | copy-start | bytes 589828
  369.9 36.9 %copy-start.38 = (f32[768]{0:T(1024)S(1)}, f32[768]{0:T(1024)}, u32[]{:S(2)}) copy-start(f32[768]{0:T(1024)} %param.27) | copy-start | bytes 9220
  369.9 36.9 %copy-start.39 = (f32[768]{0:T(1024)S(1)}, f32[768]{0:T(1024)}, u32[]{:S(2)}) copy-start(f32[768]{0:T(1024)} %param.25) | copy-start | bytes 9220
  369.9 36.9 %copy-start.42 = (f32[128]{0:T(128)S(1)}, f32[128]{0:T(128)}, u32[]{:S(2)}) copy-start(f32[128]{0:T(128)} %copy-done.41) | copy-start | bytes 1540
  369.9 36.9 %copy-start.45 = (f32[128]{0:T(128)S(1)}, f32[128]{0:T(128)}, u32[]{:S(2)}) copy-start(f32[128]{0:T(128)} %copy-done.44) | copy-start | bytes 1540
  369.9 67.2 %copy-start.46 = (f32[768]{0:T(1024)S(1)}, f32[768]{0:T(1024)}, u32[]{:S(2)}) copy-start(f32[768]{0:T(1024)} %param.36) | copy-start | bytes 9220
  369.9 67.2 %copy-start.47 = (f32[768]{0:T(1024)S(1)}, f32[768]{0:T(1024)}, u32[]{:S(2)}) copy-start(f32[768]{0:T(1024)} %param.32) | copy-start | bytes 9220
  370.9 66.3 %copy-start.30 = (bf16[128,768]{1,0:T(8,128)(2,1)S(1)}, bf16[128,768]{1,0:T(8,128)(2,1)}, u32[]{:S(2)}) copy-start(bf16[128,768]{1,0:T(8,128)(2,1)} %param.37) | copy-start | bytes 589828
  482.5 196.5 %copy-start.48 = (f32[768]{0:T(1024)}, f32[768]{0:T(1024)S(1)}, u32[]{:S(2)}) copy-start(f32[768]{0:T(1024)S(1)} %get-tuple-element.1287) | copy-start | bytes 9220
  676.0 3.0 copy-start.33
  676.0 3.8 copy-start.17
  679.8 2.5 copy-start.16
  (1 other events, 0.7 us)
Sparse Core Ops, SparseCore 0:
  26.3 45.2 all-gather.2
  74.2 42.5 all-gather.4
  182.5 164.1 reduce-scatter.6
  349.1 27.2 reduce-scatter.10
  378.7 27.9 reduce-scatter.8
  409.2 27.9 reduce-scatter.4
  442.7 232.6 all-reduce.4
where the time goes:
time: 692 us; the launch traced here: 691 us
  waiting for transfers between devices  460 us (66%)
  blocking collectives  91.1 us (13%)
  local copies, waits for them, and re-layouts  54.8 us (8%)
  matrix products  33.3 us (5%)
  other arithmetic  20.3 us (3%)
  loops' own time  16 us (2%)
  between operations  14.7 us (2%)
    psum x1, waiting for transfers between devices, local(): lax.psum((grad_qkv, qv_bias_grad, grad_dense, grad_up, grad_up_bias, grad...  193 us
    reduce_scatter x1, waiting for transfers between devices, local(): lax.psum_scatter(key_terms, 'ctx', scatter_dimension=0, tiled=True)  145 us
    all_gather x1, waiting for transfers between devices, local(): value_rows = lax.all_gather(values, 'ctx', axis=0, tiled=True)  43.7 us
    psum x1, blocking collectives, local(): lax.psum((jnp.sum(own_attn * hat_one, axis=0), jnp.sum(own_attn, axis=0),...  43 us
    all_gather x1, waiting for transfers between devices, local(): key_rows = lax.all_gather(keys_rot, 'ctx', axis=0, tiled=True)  33.9 us
    reduce_scatter x1, waiting for transfers between devices, local(): lax.psum_scatter(attn_part + mlp_part, 'tp', scatter_dimension=0, tiled=T...  28.8 us
    psum x1, blocking collectives, local(): lax.psum((grad_qkv, qv_bias_grad, grad_dense, grad_up, grad_up_bias, grad...  20.6 us
    dynamic_update_slice x8, local copies, waits for them, and re-layouts, local(): query_grad, key_terms = lax.scan(back_step, zero_query, back_inputs)  17.6 us
  transfers between devices with their start and end apart: 7, of which 6 were waited for; matrix products, arithmetic and copies ran while one was open for 5% of the time, Pallas kernels for 0%

commit v1 on v0

--- a/solution.py
+++ b/solution.py
@@ -8,6 +8,17 @@
 HD = 64
 ROT = 16
 norm_eps = 1e-05
+
+
+def collect(x, axis, dim):
+    ways = lax.axis_size(axis)
+    pieces = [x]
+    for far in range(1, ways):
+        pieces.append(
+            lax.ppermute(pieces[far - 1], axis, [(d, (d - 1) % ways) for d in range(ways)])
+        )
+    line = jnp.concatenate(pieces, axis=dim)
+    return jnp.roll(line, lax.axis_index(axis) * x.shape[dim], axis=dim)
 
 
 def layer_norm(values, scale, shift):
@@ -129,7 +140,7 @@
     )
     running = initial
     key_rows = lax.all_gather(keys_rot, "ctx", axis=0, tiled=True)
-    value_rows = lax.all_gather(values, "ctx", axis=0, tiled=True)
+    value_rows = collect(values, "ctx", 0)
     length = key_rows.shape[0]
     attend_step_rows = block_length(length)
     steps_count = length // attend_step_rows

time: 692 us -> 670 us (0.968)
  waiting for transfers between devices: 460 us -> 397 us
  starting transfers between devices: 0.29 us -> 33.6 us
  local copies, waits for them, and re-layouts: 54.8 us -> 63.6 us
    all_gather x1, waiting for transfers between devices: 43.7 us -> 9.59 us  [local(): lax.all_gather(values, 'ctx', axis=0, tiled=True)]
    all_gather x1, waiting for transfers between devices: 33.9 us -> 0.01 us  [local(): key_rows = lax.all_gather(keys_rot, 'ctx', axis=0, tiled=True)]
    ppermute x0 -> x7, starting transfers between devices: none -> 33.3 us  [collect(): lax.ppermute(pieces[far - 1], axis, [(d, (d - 1) % ways) for d in range(w...]
    ppermute x0 -> x7, waiting for transfers between devices: none -> 19 us  [collect(): lax.ppermute(pieces[far - 1], axis, [(d, (d - 1) % ways) for d in range(w...]
    reduce_scatter x1, waiting for transfers between devices: 145 us -> 132 us  [local(): lax.psum_scatter(key_terms, 'ctx', scatter_dimension=0, tiled=True)]
    unnamed x99 -> x119, local copies, waits for them, and re-layouts: 15.8 us -> 25.8 us
  transfers between devices with their start and end apart: 7 -> 14, of which waited for: 6 -> 11; matrix products, arithmetic and copies ran while one was open for 5% -> 9% of each run, Pallas kernels for 0% -> 0%
where the time goes in v1:
time: 670 us; the launch traced here: 669 us
  waiting for transfers between devices  397 us (59%)
  blocking collectives  89.9 us (13%)
  local copies, waits for them, and re-layouts  63.6 us (9%)
  matrix products  33.9 us (5%)
  starting transfers between devices  33.6 us (5%)
  other arithmetic  19.4 us (3%)
  loops' own time  16.2 us (2%)
  between operations  14.7 us (2%)
    psum x1, waiting for transfers between devices, local(): lax.psum((grad_qkv, qv_bias_grad, grad_dense, grad_up, grad_up_bias, grad...  193 us
    reduce_scatter x1, waiting for transfers between devices, local(): lax.psum_scatter(key_terms, 'ctx', scatter_dimension=0, tiled=True)  132 us
    psum x1, blocking collectives, local(): lax.psum((jnp.sum(own_attn * hat_one, axis=0), jnp.sum(own_attn, axis=0),...  43 us
    ppermute x7, starting transfers between devices, collect(): lax.ppermute(pieces[far - 1], axis, [(d, (d - 1) % ways) for d in range(w...  33.3 us
    reduce_scatter x1, waiting for transfers between devices, local(): lax.psum_scatter(attn_part + mlp_part, 'tp', scatter_dimension=0, tiled=T...  28.9 us
    unnamed x119, local copies, waits for them, and re-layouts  25.8 us
    psum x1, blocking collectives, local(): lax.psum((grad_qkv, qv_bias_grad, grad_dense, grad_up, grad_up_bias, grad...  20.7 us
    ppermute x7, waiting for transfers between devices, collect(): lax.ppermute(pieces[far - 1], axis, [(d, (d - 1) % ways) for d in range(w...  19 us
  transfers between devices with their start and end apart: 14, of which 11 were waited for; matrix products, arithmetic and copies ran while one was open for 9% of the time, Pallas kernels for 0%

profile of v1, /device:TPU:0, one launch (start us, length us, event | category | flops | bytes accessed | tf_op | source)
XLA Modules:
  0.0 668.6 jit_solution(5007538866163105697)
XLA Ops:
  7.3 1.2 convert_reduce_fusion
  9.6 1.9 fusion.74
  11.5 10.1 %all_gather.16 = bf16[512,768]{1,0:T(8,128)(2,1)S(1)} all-gather(bf16[128,768]{1,0:T(8,128)(2,1)S(1)} %get-tuple-element.958), channel_id=1, replica_groups=mesh['ctx'=8,'tp'=4] {'tp'}, dimensions={0}, use_global_device_ids=true | all-gather | bytes 983040 | tf_op jit(solution)/shard_map/all_gather | solution.py:89
  25.5 1.6 pad_maximum_fusion.1
  28.1 4.5 collective-permute-start
  32.7 5.8 collective-permute-done
  38.5 5.2 collective-permute-start.1
  43.7 7.4 %all_gather.20 = bf16[512,768]{1,0:T(8,128)(2,1)S(1)} all-gather(bf16[128,768]{1,0:T(8,128)(2,1)} %param.37), channel_id=1, replica_groups=mesh['ctx'=8,'tp'=4] {'tp'}, dimensions={0}, use_global_device_ids=true | all-gather | bytes 983040 | tf_op jit(solution)/shard_map/all_gather | solution.py:180
  51.2 3.5 collective-permute-start.2
  55.2 3.1 collective-permute-done.2
  58.4 4.6 collective-permute-start.3
  64.1 4.6 collective-permute-done.3
  68.7 5.2 collective-permute-start.4
  75.4 1.9 collective-permute-done.4
  77.3 5.1 collective-permute-start.5
  83.9 1.7 collective-permute-done.5
  85.6 5.2 collective-permute-start.6
  92.2 1.7 collective-permute-done.6
  100.5 1.5 constant_dynamic-slice_fusion
  102.1 1.3 copy.76
  103.4 1.6 copy.77
  105.0 16.9 %while.39 = (s32[]{:T(128)}, f32[3,512]{1,0:T(4,128)S(1)}, f32[3,512]{1,0:T(4,128)S(1)}, f32[3,512,64]{1,2,0:T(8,128)S(1)}, s32[4]{0:T(128)S(1)}, /*index=5*/s32...) while((s32[]{:T(128)}, f32[3,512]{1,0:T(4,128)S(1)}, ...), condition=%wide.region_8.9_spmd.clone, body=%wide.region_3.8_spmd.clone.sunk | while | flops 424874496 | bytes 22858608 | solution.py:165
  107.6 6.5 conditional.6
  108.1 1.4 fusion.4
  109.5 1.6 fusion.6
  111.1 3.0 fusion.10
  121.9 9.6 %all-gather.5.cloned.1.call-done = bf16[4096,3,64]{0,2,1:T(8,128)(2,1)} async-done(((bf16[512,3,64]{0,2,1:T(8,128)(2,1)}), bf16[4096,3,64]{0,2,1:T(8,128)(2,1)}) %all-gather.5.cloned.1.call-update) | async-done | bytes 1572880 | tf_op jit(solution)/shard_map/all_gather | solution.py:209
  131.5 2.8 copy.75
  134.8 1.4 multiply_reduce_fusion
  136.3 37.3 %while.40 = (s32[]{:T(128)}, f32[512,3,64]{0,2,1:T(8,128)S(1)}, f32[4,1024,384]{2,1,0:T(8,128)}, s32[4]{0:T(128)S(1)}, s32[]{:T(128)}, /*index=5*/s32[]{:T(128)}...) while((s32[]{:T(128)}, f32[512,3,64]{0,2,1:T(8,128)S(1)}, ...), condition=%wide.region_14.15_spmd.clone, body=%wide.region_11.14_spmd.clone.sunk | while | flops 1024722432 | bytes 56325616 | solution.py:258
  138.9 8.3 %conditional.7 = (f32[512,3,64]{0,2,1:T(8,128)S(1)}, f32[1,1024,384]{1,2,0:T(8,128)S(1)}) conditional(s32[]{:T(128)} %convert_element_type.209, f32[512,3,64]{0,2,1:T(8,128)S(1)} %get-tuple-element.1217, (s32[]{:T(128)}, s32[]{:T(128)}, s32[512]{0:T(512)}, bf16[4,1024,3,64]{1,3,2,0:T(8,128)(2,1)S(1)}, s32[]{:T(128)}, ...), branch_computations={%region_12.12_spmd, %region_13.13_spmd} | conditional | flops 1024722432 | bytes 37448308 | solution.py:256
  140.5 3.3 fusion.23
  144.6 1.5 fusion.25
  147.3 1.6 copy.79
  148.9 2.8 constant_dynamic-update-slice_fusion.18
  154.6 1.6 copy.79
  156.2 2.8 constant_dynamic-update-slice_fusion.18
  161.8 1.6 copy.79
  163.4 2.8 constant_dynamic-update-slice_fusion.18
  169.1 1.6 copy.79
  170.7 2.8 constant_dynamic-update-slice_fusion.18
  174.5 8.8 %all_gather.18 = bf16[512,768]{1,0:T(8,128)(2,1)S(1)} all-gather(bf16[128,768]{1,0:T(8,128)(2,1)S(1)} %copy-done.33), channel_id=1, replica_groups=mesh['ctx'=8,'tp'=4] {'tp'}, dimensions={0}, use_global_device_ids=true | all-gather | bytes 983040 | tf_op jit(solution)/shard_map/all_gather | solution.py:90
  183.3 4.2 fusion.44
  189.5 2.0 fusion.93
  193.1 131.7 %reduce-scatter.7.cloned.1.call-done = f32[512,384]{1,0:T(8,128)} async-done(((f32[4096,384]{1,0:T(8,128)}), f32[512,384]{1,0:T(8,128)}) %reduce-scatter.7.cloned.1.call-update) | async-done | bytes 786448 | tf_op jit(solution)/shard_map/reduce_scatter | solution.py:260
  324.7 2.0 slice.122
  326.7 1.8 copy.46
  329.4 1.3 copy.45
  332.6 2.0 fusion.112
  336.0 1.9 convolution_add_fusion
  339.0 3.3 fusion.91
  342.4 2.2 fusion.114
  344.6 1.1 fusion.113
  346.1 1.8 fusion.59
  349.1 20.7 %all-reduce.1 = (f32[2,192]{1,0:T(2,128)}, f32[768]{0:T(1024)}) all-reduce(f32[2,192]{1,0:T(2,128)S(1)} %pad_maximum_fusion.4, f32[768]{0:T(1024)S(1)} %get-tuple-element.970), channel_id=1, replica_groups=mesh['ctx'=8,'tp'=4] {'ctx'}, use_global_device_ids=true, to_apply=%region_33.34 | all-reduce | flops 1152 | bytes 9216 | tf_op jit(solution)/shard_map/psum | solution.py:295
  369.8 15.1 %reduce-scatter.9.cloned.1.call-done = f32[128,768]{1,0:T(8,128)} async-done(((f32[512,768]{1,0:T(8,128)}), f32[128,768]{1,0:T(8,128)}) %reduce-scatter.9.cloned.1.call-update) | async-done | bytes 393232 | tf_op jit(solution)/shard_map/reduce_scatter | solution.py:280
  384.9 1.5 fusion.82
  386.4 28.9 %reduce-scatter.5.cloned.1.call-done = f32[128,768]{1,0:T(8,128)} async-done(((f32[512,768]{1,0:T(8,128)}), f32[128,768]{1,0:T(8,128)}) %reduce-scatter.5.cloned.1.call-update) | async-done | bytes 393232 | tf_op jit(solution)/shard_map/reduce_scatter | solution.py:176
  415.3 2.3 convert_reduce_fusion.1
  417.6 43.0 %all-reduce = (f32[768]{0:T(1024)}, f32[768]{0:T(1024)}, f32[768]{0:T(1024)}, f32[768]{0:T(1024)}, f32[768]{0:T(1024)S(1)}) all-reduce(f32[768]{0:T(1024)S(1)} %get-tuple-element.862, f32[768]{0:T(1024)S(1)} %get-tuple-element.867, f32[768]{0:T(1024)S(1)} %get-tuple-element.871, ...), channel_id=1, replica_groups=mesh['ctx'=8,'tp'=4] {'ctx','tp'}, use_global_device_ids=true, to_apply=%region_23.24 | all-reduce | flops 3840 | bytes 30720 | tf_op jit(solution)/shard_map/psum | solution.py:285
  460.5 193.0 %all-reduce.5.cloned.1.call-done = (f32[768,3,192]{0,2,1:T(8,128)}, f32[192,768]{1,0:T(8,128)}, f32[768,768]{1,0:T(8,128)}, f32[768,768]{1,0:T(8,128)}) async-done(((f32[768,3,192]{0,2,1:T(8,128)}, f32[192,768]{1,0:T(8,128)}, f32[768,768]{1,0:T(8,128)}, f32[768,768]{1,0:T(8,128)}), (f32[768,3,192]{0,2,1:T(8,128)}, f32[192,768]{1,0:T(8,128)}, f32[768,768]{1,0:T(8,128)}, ...) | async-done | bytes 7077904 | tf_op jit(solution)/shard_map/psum | solution.py:295
  654.1 2.9 copy.135
  657.9 1.4 copy.137
  660.4 1.4 copy.138
  (243 shorter events, 43.2 us)
Async XLA Ops:
  7.2 176.1 %copy-start = (bf16[768,768]{1,0:T(8,128)(2,1)S(1)}, bf16[768,768]{1,0:T(8,128)(2,1)}, u32[]{:S(2)}) copy-start(bf16[768,768]{1,0:T(8,128)(2,1)} %param.33) | copy-start | bytes 3538948
  7.2 14.4 %copy-start.12 = (bf16[768,3,192]{0,2,1:T(8,128)(2,1)S(1)}, bf16[768,3,192]{0,2,1:T(8,128)(2,1)}, u32[]{:S(2)}) copy-start(bf16[768,3,192]{0,2,1:T(8,128)(2,1)} %param.29) | copy-start | bytes 2654212
  7.2 96.2 %all-gather.3.cloned.1.call-start = ((), (), s32[]{:S(2)}) async-start(), calls=%async_computation.4 | async-start | bytes 1769472 | tf_op jit(solution)/shard_map/all_gather | solution.py:142
  8.5 13.1 %copy-start.44 = (f32[128]{0:T(128)}, f32[128]{0:T(128)S(1)}, u32[]{:S(2)}) copy-start(f32[128]{0:T(128)S(1)} %broadcast_multiply_fusion.5) | copy-start | bytes 1540
  9.6 12.0 %copy-start.47 = (f32[128]{0:T(128)}, f32[128]{0:T(128)S(1)}, u32[]{:S(2)}) copy-start(f32[128]{0:T(128)S(1)} %add_rsqrt_fusion) | copy-start | bytes 1540
  21.6 1.6 copy-start.53
  22.2 1.2 copy-start.52
  25.5 37.6 %copy-start.25 = (bf16[192,768]{1,0:T(8,128)(2,1)S(1)}, bf16[192,768]{1,0:T(8,128)(2,1)}, u32[]{:S(2)}) copy-start(bf16[192,768]{1,0:T(8,128)(2,1)} %param.31) | copy-start | bytes 884740
  27.1 104.4 %all-gather.5.cloned.1.call-start = ((), (), s32[]{:S(2)}) async-start(), calls=%async_computation.6 | async-start | bytes 1769472 | tf_op jit(solution)/shard_map/all_gather | solution.py:209
  28.1 4.5 copy-start.19
  28.1 10.4 %collective-permute-start = (bf16[512,3,64]{0,2,1:T(8,128)(2,1)S(1)}, bf16[512,3,64]{0,2,1:T(8,128)(2,1)S(1)}, u32[]{:S(2)}, u32[]{:S(2)}) collective-permute-start(bf16[512,3,64]{0,2,1:T(8,128)(2,1)S(1)} %get-tuple-element.942), channel_id=1, source_target_pairs={{0,28},{4,0},{8,4},{12,8},{16,12},{20,16},{24,20},{28,24},{1,29},{... | collective-permute-start | bytes 589832 | tf_op jit(solution)/shard_map/ppermute | solution.py:18
  32.6 292.1 %reduce-scatter.7.cloned.1.call-start = ((), (), s32[]{:S(2)}) async-start(), calls=%async_computation.7 | async-start | bytes 7077888 | tf_op jit(solution)/shard_map/reduce_scatter | solution.py:260
  38.5 12.6 %collective-permute-start.1 = (bf16[512,3,64]{0,2,1:T(8,128)(2,1)S(1)}, bf16[512,3,64]{0,2,1:T(8,128)(2,1)S(1)}, u32[]{:S(2)}, u32[]{:S(2)}) collective-permute-start(bf16[512,3,64]{0,2,1:T(8,128)(2,1)S(1)} %collective-permute-done), channel_id=1, source_target_pairs={{0,28},{4,0},{8,4},{12,8},{16,12},{20,16},{24,20},{28,24},{1,29},{... | collective-permute-start | bytes 589832 | tf_op jit(solution)/shard_map/ppermute | solution.py:18
  51.1 32.0 %copy-start.3 = (bf16[512,768]{1,0:T(8,128)(2,1)}, bf16[512,768]{1,0:T(8,128)(2,1)S(1)}, u32[]{:S(2)}) copy-start(bf16[512,768]{1,0:T(8,128)(2,1)S(1)} %all_gather.20) | copy-start | bytes 2359300
  51.2 7.2 %collective-permute-start.2 = (bf16[512,3,64]{0,2,1:T(8,128)(2,1)S(1)}, bf16[512,3,64]{0,2,1:T(8,128)(2,1)S(1)}, u32[]{:S(2)}, u32[]{:S(2)}) collective-permute-start(bf16[512,3,64]{0,2,1:T(8,128)(2,1)S(1)} %collective-permute-done.1), channel_id=1, source_target_pairs={{0,28},{4,0},{8,4},{12,8},{16,12},{20,16},{24,20},{28,24},{1,29},{... | collective-permute-start | bytes 589832 | tf_op jit(solution)/shard_map/ppermute | solution.py:18
  58.4 10.4 %collective-permute-start.3 = (bf16[512,3,64]{0,2,1:T(8,128)(2,1)S(1)}, bf16[512,3,64]{0,2,1:T(8,128)(2,1)S(1)}, u32[]{:S(2)}, u32[]{:S(2)}) collective-permute-start(bf16[512,3,64]{0,2,1:T(8,128)(2,1)S(1)} %collective-permute-done.2), channel_id=1, source_target_pairs={{0,28},{4,0},{8,4},{12,8},{16,12},{20,16},{24,20},{28,24},{1,29},{... | collective-permute-start | bytes 589832 | tf_op jit(solution)/shard_map/ppermute | solution.py:18
  64.1 30.6 %copy-start.20 = (bf16[512,3,64]{0,2,1:T(8,128)(2,1)S(1)}, bf16[512,3,64]{0,2,1:T(8,128)(2,1)}, u32[]{:S(2)}) copy-start(bf16[512,3,64]{0,2,1:T(8,128)(2,1)} %copy-done.19) | copy-start | bytes 589828
  68.7 8.6 %collective-permute-start.4 = (bf16[512,3,64]{0,2,1:T(8,128)(2,1)S(1)}, bf16[512,3,64]{0,2,1:T(8,128)(2,1)S(1)}, u32[]{:S(2)}, u32[]{:S(2)}) collective-permute-start(bf16[512,3,64]{0,2,1:T(8,128)(2,1)S(1)} %collective-permute-done.3), channel_id=1, source_target_pairs={{0,28},{4,0},{8,4},{12,8},{16,12},{20,16},{24,20},{28,24},{1,29},{... | collective-permute-start | bytes 589832 | tf_op jit(solution)/shard_map/ppermute | solution.py:18
  77.3 8.3 %collective-permute-start.5 = (bf16[512,3,64]{0,2,1:T(8,128)(2,1)S(1)}, bf16[512,3,64]{0,2,1:T(8,128)(2,1)S(1)}, u32[]{:S(2)}, u32[]{:S(2)}) collective-permute-start(bf16[512,3,64]{0,2,1:T(8,128)(2,1)S(1)} %collective-permute-done.4), channel_id=1, source_target_pairs={{0,28},{4,0},{8,4},{12,8},{16,12},{20,16},{24,20},{28,24},{1,29},{... | collective-permute-start | bytes 589832 | tf_op jit(solution)/shard_map/ppermute | solution.py:18
  85.6 8.4 %collective-permute-start.6 = (bf16[512,3,64]{0,2,1:T(8,128)(2,1)S(1)}, bf16[512,3,64]{0,2,1:T(8,128)(2,1)S(1)}, u32[]{:S(2)}, u32[]{:S(2)}) collective-permute-start(bf16[512,3,64]{0,2,1:T(8,128)(2,1)S(1)} %collective-permute-done.5), channel_id=1, source_target_pairs={{0,28},{4,0},{8,4},{12,8},{16,12},{20,16},{24,20},{28,24},{1,29},{... | collective-permute-start | bytes 589832 | tf_op jit(solution)/shard_map/ppermute | solution.py:18
  121.9 9.6 %copy-start.39 = (s32[512]{0:T(512)}, s32[512]{0:T(512)S(1)}, u32[]{:S(2)}) copy-start(s32[512]{0:T(512)S(1)} %get-tuple-element.1354) | copy-start | bytes 6148
  131.5 3.4 copy-start.30
  136.3 2.6 copy-start.1
  138.9 1.1 copy-start.40
  139.0 1.6 copy-start.43
  139.0 1.6 copy-start.46
  148.9 2.8 copy-start.2
  151.7 2.6 copy-start.1
  156.2 2.8 copy-start.2
  159.0 2.6 copy-start.1
  163.4 2.8 copy-start.2
  166.2 2.6 copy-start.1
  170.7 2.8 copy-start.2
  173.5 9.7 %copy-start.54 = (f32[768]{0:T(1024)S(1)}, f32[768]{0:T(1024)}, u32[]{:S(2)}) copy-start(f32[768]{0:T(1024)} %param.34) | copy-start | bytes 9220
  173.6 196.2 %reduce-scatter.11.cloned.1.call-start = ((), (), s32[]{:S(2)}) async-start(), calls=%async_computation.9 | async-start | bytes 1966080 | tf_op jit(solution)/shard_map/reduce_scatter | solution.py:281
  183.3 4.3 copy-start.7
  183.3 4.3 copy-start.4
  183.3 4.3 copy-start.23
  191.6 193.3 %reduce-scatter.9.cloned.1.call-start = ((), (), s32[]{:S(2)}) async-start(), calls=%async_computation.8 | async-start | bytes 1966080 | tf_op jit(solution)/shard_map/reduce_scatter | solution.py:280
  324.7 3.7 copy-start.18
  329.4 2.2 copy-start.29
  329.4 2.3 copy-start.31
  330.7 1.9 copy-start.13
  332.6 2.1 copy-start.21
  332.6 2.1 copy-start.26
  334.6 80.6 %reduce-scatter.5.cloned.1.call-start = ((), (), s32[]{:S(2)}) async-start(), calls=%async_computation.5 | async-start | bytes 1966080 | tf_op jit(solution)/shard_map/reduce_scatter | solution.py:176
  334.7 1.3 copy-start.24
  337.9 1.1 copy-start.8
  337.9 315.6 %all-reduce.5.cloned.1.call-start = ((), (), s32[]{:S(2)}) async-start(), calls=%async_computation.10 | async-start | bytes 14155776 | tf_op jit(solution)/shard_map/psum | solution.py:295
  342.4 2.2 copy-start.22
  344.6 1.2 copy-start.6
  344.6 1.5 copy-start.10
  347.9 36.9 %copy-start.11 = (bf16[128,768]{1,0:T(8,128)(2,1)S(1)}, bf16[128,768]{1,0:T(8,128)(2,1)}, u32[]{:S(2)}) copy-start(bf16[128,768]{1,0:T(8,128)(2,1)} %param.23) | copy-start | bytes 589828
  347.9 36.9 %copy-start.41 = (f32[768]{0:T(1024)S(1)}, f32[768]{0:T(1024)}, u32[]{:S(2)}) copy-start(f32[768]{0:T(1024)} %param.27) | copy-start | bytes 9220
  347.9 36.9 %copy-start.42 = (f32[768]{0:T(1024)S(1)}, f32[768]{0:T(1024)}, u32[]{:S(2)}) copy-start(f32[768]{0:T(1024)} %param.25) | copy-start | bytes 9220
  347.9 36.9 %copy-start.45 = (f32[128]{0:T(128)S(1)}, f32[128]{0:T(128)}, u32[]{:S(2)}) copy-start(f32[128]{0:T(128)} %copy-done.44) | copy-start | bytes 1540
  347.9 36.9 %copy-start.48 = (f32[128]{0:T(128)S(1)}, f32[128]{0:T(128)}, u32[]{:S(2)}) copy-start(f32[128]{0:T(128)} %copy-done.47) | copy-start | bytes 1540
  347.9 67.3 %copy-start.49 = (f32[768]{0:T(1024)S(1)}, f32[768]{0:T(1024)}, u32[]{:S(2)}) copy-start(f32[768]{0:T(1024)} %param.36) | copy-start | bytes 9220
  348.0 67.3 %copy-start.50 = (f32[768]{0:T(1024)S(1)}, f32[768]{0:T(1024)}, u32[]{:S(2)}) copy-start(f32[768]{0:T(1024)} %param.32) | copy-start | bytes 9220
  348.9 66.4 %copy-start.32 = (bf16[128,768]{1,0:T(8,128)(2,1)S(1)}, bf16[128,768]{1,0:T(8,128)(2,1)}, u32[]{:S(2)}) copy-start(bf16[128,768]{1,0:T(8,128)(2,1)} %param.37) | copy-start | bytes 589828
  460.5 196.5 %copy-start.51 = (f32[768]{0:T(1024)}, f32[768]{0:T(1024)S(1)}, u32[]{:S(2)}) copy-start(f32[768]{0:T(1024)S(1)} %get-tuple-element.1287) | copy-start | bytes 9220
  654.1 3.0 copy-start.35
  654.1 3.8 copy-start.17
  657.9 2.5 copy-start.16
  (11 other events, 9.1 us)
Sparse Core Ops, SparseCore 0:
  27.2 56.6 all-gather.2
  86.6 44.8 all-gather.4
  173.7 151.0 reduce-scatter.6
  327.1 27.2 reduce-scatter.10
  356.8 27.9 reduce-scatter.8
  387.2 27.9 reduce-scatter.4
  420.8 232.6 all-reduce.4
